TPU v7x, 128 devices: a whole 4x4x4 slice. The times are simulated.
128 devices in a mesh: gx: 8 (over x, core), gy: 16 (over y, z).
Axes of the slice: x: 4, y: 4, z: 4, core: 2. Of those that a mesh axis runs over, the one named last changes fastest.
Arguments:
- point_coords: float32 [3, 2097152], P(None, ('gx', 'gy')), may hold values from -1 to 1
- strengths: float32 [3, 2097152], P(None, ('gx', 'gy')), may hold values from -0.06 to 0.06
- centers: float32 [3, 2048], replicated, may hold values from 0 to 0.3
- half_widths: float32 [2048], replicated, may hold values from 0.1 to 0.3
- tile_source: int32 [128, 128], P(('gx', 'gy')), may hold values from 0 to 2047, as said below
- tile_target: int32 [128, 128], P(('gx', 'gy')), may hold values from 0 to 2047, as said below
- tile_count: int32 [128], P(('gx', 'gy')), may hold values from 1 to 128, as said below
Outputs:
- velocity: float32 [3, 2097152], P(None, ('gx', 'gy'))
Inputs may be any that keep to these rules, and one draw needn't show every extreme that they name: `tile_source`: cluster c belongs to domain c // 16. Among the first tile_count[d] entries of row d at most 1 name clusters of any one domain, and some domain reaches 1; later entries are valid ids of no interaction. `tile_target`: cluster c belongs to domain c // 16. Among the first tile_count[d] entries of row d at most 1 name clusters of any one domain, and some domain reaches 1; later entries are valid ids of no interaction. `tile_count`: 128 on at least one domain.
All inputs are finite; a program needn't handle non-finite values.
Results may differ from a plain program's by a relative error of at most 0.0001.
Values sent between devices are 32-bit elements; how exact they have to be, the bound alone decides.
No kernel may reach another device: no remote copies, remote signals or barrier semaphores. Data moves between devices by JAX's collectives and lax.ppermute only.
A program may use at most 64 MiB of HBM per device.

v0:
```python
import jax
import jax.numpy as jnp
from jax import lax
from jax.sharding import PartitionSpec as P

CL_DEV = 16
PTS = 1024
DEG = 7
TILES_DEV = 128


smoothing_sq = 0.01
biot_factor = -0.07957747154594767


def chebyshev(degree):
    counter = jnp.arange(degree + 1, dtype=jnp.float32)
    return jnp.cos(jnp.pi * counter / degree)


def lagrange(points, cheb_nodes):
    node_count = cheb_nodes.shape[0]
    differ = points[None, :] - cheb_nodes[:, None]
    diagonal = jnp.eye(node_count, dtype=bool)
    numerator = jnp.prod(jnp.where(diagonal[:, :, None], 1.0, differ[None, :, :]), axis=1)
    spacing = cheb_nodes[:, None] - cheb_nodes[None, :]
    denominator = jnp.prod(jnp.where(diagonal, 1.0, spacing), axis=1)
    return numerator / denominator[:, None]


def basis_parts(coords, cheb_nodes):
    basis_x = lagrange(coords[0], cheb_nodes)
    basis_y = lagrange(coords[1], cheb_nodes)
    basis_z = lagrange(coords[2], cheb_nodes)
    node_count = cheb_nodes.shape[0]
    paired = (basis_y[:, None, :] * basis_z[None, :, :]).reshape(node_count * node_count, -1)
    return (basis_x, paired)


def upward(coords, weights, cheb_nodes):
    basis_x, paired = basis_parts(coords, cheb_nodes)
    weighted = weights[:, None, :] * paired[None, :, :]
    charge = jnp.einsum("ai,cei->cae", basis_x, weighted, precision=lax.Precision.HIGHEST)
    return charge.reshape(3, -1)


def downward(coords, proxy_values, cheb_nodes):
    basis_x, paired = basis_parts(coords, cheb_nodes)
    node_count = cheb_nodes.shape[0]
    shaped = proxy_values.reshape(3, node_count, node_count * node_count)
    spread = jnp.einsum("cae,ai->cei", shaped, basis_x, precision=lax.Precision.HIGHEST)
    return jnp.sum(spread * paired[None, :, :], axis=1)


def proxy_grid(center, half_width, cheb_nodes):
    node_count = cheb_nodes.shape[0]
    cube_shape = (node_count, node_count, node_count)
    along_x = jnp.broadcast_to(cheb_nodes[:, None, None], cube_shape).reshape(-1)
    along_y = jnp.broadcast_to(cheb_nodes[None, :, None], cube_shape).reshape(-1)
    along_z = jnp.broadcast_to(cheb_nodes[None, None, :], cube_shape).reshape(-1)
    return center[:, None] + half_width * jnp.stack([along_x, along_y, along_z])


def features_of(charge, grid_points):
    return jnp.stack(
        [
            charge[0],
            charge[1],
            charge[2],
            grid_points[1] * charge[2],
            grid_points[2] * charge[1],
            grid_points[2] * charge[0],
            grid_points[0] * charge[2],
            grid_points[0] * charge[1],
            grid_points[1] * charge[0],
        ]
    )


def tile_from_features(target_grid, source_grid, feature_rows):
    offset = target_grid[:, None, :] - source_grid[:, :, None]
    radius_sq = jnp.sum(offset * offset, axis=0) + smoothing_sq
    kernel = 1.0 / (radius_sq * jnp.sqrt(radius_sq))
    summed = jnp.dot(
        feature_rows, kernel, precision=lax.Precision.HIGHEST, preferred_element_type=jnp.float32
    )
    velocity_x = target_grid[1] * summed[2] - summed[3] - target_grid[2] * summed[1] + summed[4]
    velocity_y = target_grid[2] * summed[0] - summed[5] - target_grid[0] * summed[2] + summed[6]
    velocity_z = target_grid[0] * summed[1] - summed[7] - target_grid[1] * summed[0] + summed[8]
    return biot_factor * jnp.stack([velocity_x, velocity_y, velocity_z])


def slot_layout(cluster_ids, alive_mask, capacity, slot_total):
    owners = cluster_ids // CL_DEV
    local_id = cluster_ids % CL_DEV
    positions = jnp.arange(cluster_ids.shape[0])
    earlier = (
        (owners[None, :] == owners[:, None])
        & alive_mask[None, :]
        & (positions[None, :] < positions[:, None])
    )
    tile_rank = jnp.minimum(jnp.sum(earlier.astype(jnp.int32), axis=1), capacity - 1)
    slot_of = owners * capacity + tile_rank
    matches = (jnp.arange(slot_total)[:, None] == slot_of[None, :]) & alive_mask[None, :]
    slot_table = jnp.sum(jnp.where(matches, local_id[None, :] + 1, 0), axis=1) - 1
    return (slot_of, slot_table)


def local(point_coords, strengths, centers, half_widths, tile_source, tile_target, tile_count):
    domains = lax.axis_size(("gx", "gy"))
    capacity = (TILES_DEV + domains - 1) // domains
    slot_total = capacity * domains
    cheb_nodes = chebyshev(DEG)
    proxy_count = (DEG + 1) ** 3
    coords = point_coords.reshape(3, CL_DEV, PTS).transpose(1, 0, 2)
    weights = strengths.reshape(3, CL_DEV, PTS).transpose(1, 0, 2)
    charges = lax.map(lambda pieces: upward(pieces[0], pieces[1], cheb_nodes), (coords, weights))
    make_grid = jax.vmap(lambda center, half_width: proxy_grid(center, half_width, cheb_nodes))
    offered = charges.reshape(CL_DEV, 3 * proxy_count)
    row_count = 3
    tile_total = tile_count[0]
    source_ids = tile_source[0]
    target_ids = tile_target[0]
    alive_mask = jnp.arange(TILES_DEV) < tile_total
    source_slots, requests = slot_layout(source_ids, alive_mask, capacity, slot_total)
    target_slots, receivers = slot_layout(target_ids, alive_mask, capacity, slot_total)
    asked_for = lax.all_to_all(requests, ("gx", "gy"), split_axis=0, concat_axis=0, tiled=True)
    selector = (asked_for[:, None] == jnp.arange(CL_DEV)[None, :]).astype(jnp.float32)
    answer = jnp.dot(
        selector, offered, precision=lax.Precision.HIGHEST, preferred_element_type=jnp.float32
    )
    fetched = lax.all_to_all(answer, ("gx", "gy"), split_axis=0, concat_axis=0, tiled=True)

    def add_group(group_step, outgoing):
        first_tile = group_step * 8
        group_sources = lax.dynamic_slice_in_dim(source_ids, first_tile, 8)
        group_targets = lax.dynamic_slice_in_dim(target_ids, first_tile, 8)
        group_source_slots = lax.dynamic_slice_in_dim(source_slots, first_tile, 8)
        group_target_slots = lax.dynamic_slice_in_dim(target_slots, first_tile, 8)
        source_grid = make_grid(
            jnp.take(centers, group_sources, axis=1).T, jnp.take(half_widths, group_sources)
        )
        target_grid = make_grid(
            jnp.take(centers, group_targets, axis=1).T, jnp.take(half_widths, group_targets)
        )
        fetched_rows = jnp.take(fetched, group_source_slots, axis=0).reshape(
            8, row_count, proxy_count
        )
        feature_rows = jax.vmap(features_of)(fetched_rows, source_grid)
        contrib = jax.vmap(tile_from_features)(target_grid, source_grid, feature_rows)
        alive_rows = (first_tile + jnp.arange(8) < tile_total).astype(jnp.float32)
        return outgoing.at[group_target_slots].add(contrib.reshape(8, -1) * alive_rows[:, None])

    outgoing = jnp.zeros((slot_total, 3 * proxy_count), jnp.float32)
    outgoing = lax.fori_loop(0, (tile_total + 7) // 8, add_group, outgoing)
    parts_recv, senders = (
        lax.all_to_all(outgoing, ("gx", "gy"), split_axis=0, concat_axis=0, tiled=True),
        lax.all_to_all(receivers, ("gx", "gy"), split_axis=0, concat_axis=0, tiled=True),
    )
    assign = (jnp.arange(CL_DEV)[:, None] == senders[None, :]).astype(jnp.float32)
    proxy_velocity = jnp.dot(
        assign, parts_recv, precision=lax.Precision.HIGHEST, preferred_element_type=jnp.float32
    )
    proxy_velocity = proxy_velocity.reshape(CL_DEV, 3, proxy_count)
    velocity = lax.map(
        lambda pieces: downward(pieces[0], pieces[1], cheb_nodes), (coords, proxy_velocity)
    )
    return velocity.transpose(1, 0, 2).reshape(3, CL_DEV * PTS)


def solution(mesh):
    return jax.shard_map(
        local,
        mesh=mesh,
        in_specs=(
            P(None, ("gx", "gy")),
            P(None, ("gx", "gy")),
            P(),
            P(),
            P(("gx", "gy"), None),
            P(("gx", "gy"), None),
            P(("gx", "gy")),
        ),
        out_specs=P(None, ("gx", "gy")),
        check_vma=False,
    )
```

profile of v0, /device:TPU:1, one launch (start us, length us, event | category | flops | bytes accessed | tf_op | source)
XLA Modules:
  0.0 559.6 jit_solution(17969634036640111805)
XLA Ops:
  4.7 11.5 %all-to-all-start.1 = ((s32[128,1,1]{2,1,0:T(1,128)}), s32[128,1,1]{2,1,0:T(1,128)S(1)}, u32[]{:S(2)}, u32[]{:S(2)}) async-start(s32[128,1,1]{2,1,0:T(1,128)} %copy.31), calls=%async_computation.1 | async-start | bytes 131072 | tf_op jit(solution)/shard_map/all_to_all | solution.py:127
  16.2 53.5 %while.36 = (s32[]{:T(128)}, f32[16,3,512]{2,1,0:T(4,128)S(1)}, f32[16,3,1024]{2,1,0:T(4,128)}, f32[16,3,1024]{2,1,0:T(4,128)}, s32[]{:T(128)}, /*index=5*/s32[]{:T(128)}, s32[]{}, s32[]{}) while((s32[]{:T(128)}, f32[16,3,512]{2,1,0:T(4,128)S(1)}, f32[16,3,1024]{2,1,0:T(4,128)}, f32[16,3,1024]{2,1,0:T(4,128)}, ...), condition=%wide.region_9.10_spmd.clone.clone, body=%wide.region_4.9_spmd.clone.clone.sunk | while | flops 19554628 | bytes 1157569 | solution.py:117
  18.5 0.9 convolution_bitcast_fusion.3
  28.5 0.9 convolution_bitcast_fusion.3
  31.9 0.9 convolution_bitcast_fusion.3
  69.7 2.4 reduce.1
  72.6 1.7 copy.32
  74.3 9.8 %all-to-all-start.2 = ((f32[128,1,1536]{2,1,0:T(1,128)}), f32[128,1,1536]{2,1,0:T(1,128)S(1)}, u32[]{:S(2)}, u32[]{:S(2)}) async-start(f32[128,1,1536]{2,1,0:T(1,128)} %copy.32), calls=%async_computation.2 | async-start | bytes 1572864 | tf_op jit(solution)/shard_map/all_to_all | solution.py:132
  85.3 15.3 %all-to-all-done.2 = f32[128,1,1536]{2,1,0:T(1,128)S(1)} async-done(((f32[128,1,1536]{2,1,0:T(1,128)}), f32[128,1,1536]{2,1,0:T(1,128)S(1)}, u32[]{:S(2)}, u32[]{:S(2)}) %all-to-all-start.2) | async-done | bytes 786464 | tf_op jit(solution)/shard_map/all_to_all | solution.py:132
  100.6 4.3 all-to-all-start
  105.0 383.6 %while.37 = (s32[]{:T(128)}, f32[128,1536]{1,0:T(8,128)S(1)}, s32[]{:T(128)}, s32[128]{0:T(128)S(1)}, s32[128]{0:T(128)S(1)}, /*index=5*/f32[3,2048]{0,1:T(8,128...) while((s32[]{:T(128)}, f32[128,1536]{1,0:T(8,128)S(1)}, ...), condition=%wide.region_13.16_spmd.clone.clone, body=%wide.region_10.15_spmd.clone.clone.sunk | while | flops 249776448 | bytes 19483360 | solution.py:155
  108.5 7.1 %multiply_reduce_fusion.2 = f32[8,512,512]{2,1,0:T(8,128)} fusion(f32[8,3,512]{2,1,0:T(4,128)S(1)} %get-tuple-element.594, f32[8,3,512]{2,1,0:T(4,128)S(1)} %get-tuple-element.595), kind=kLoop, calls=%fused_computation.55.clone.1 | loop fusion | flops 16777216 | bytes 8486912 | tf_op jit(solution)/shard_map/while/body/vmap()/reduce_sum | solution.py:82
  117.4 10.4 %fusion.76 = f32[8,9,512]{2,1,0:T(8,128)S(1)} fusion(f32[8,512,512]{2,1,0:T(8,128)} %multiply_reduce_fusion.2, f32[9,8,512]{2,0,1:T(8,128)S(1)} %stack.26), kind=kOutput, calls=%fused_computation.58.clone.1 | convolution fusion | flops 232783872 | bytes 8683520 | tf_op jit(solution)/shard_map/while/body/vmap()/dot_general | solution.py:84
  128.1 1.0 scatter_custom_fusion.6
  132.4 7.1 %multiply_reduce_fusion.2 = f32[8,512,512]{2,1,0:T(8,128)} fusion(f32[8,3,512]{2,1,0:T(4,128)S(1)} %get-tuple-element.594, f32[8,3,512]{2,1,0:T(4,128)S(1)} %get-tuple-element.595), kind=kLoop, calls=%fused_computation.55.clone.1 | loop fusion | flops 16777216 | bytes 8486912 | tf_op jit(solution)/shard_map/while/body/vmap()/reduce_sum | solution.py:82
  141.4 10.4 %fusion.76 = f32[8,9,512]{2,1,0:T(8,128)S(1)} fusion(f32[8,512,512]{2,1,0:T(8,128)} %multiply_reduce_fusion.2, f32[9,8,512]{2,0,1:T(8,128)S(1)} %stack.26), kind=kOutput, calls=%fused_computation.58.clone.1 | convolution fusion | flops 232783872 | bytes 8683520 | tf_op jit(solution)/shard_map/while/body/vmap()/dot_general | solution.py:84
  152.1 1.0 scatter_custom_fusion.6
  156.4 7.1 %multiply_reduce_fusion.2 = f32[8,512,512]{2,1,0:T(8,128)} fusion(f32[8,3,512]{2,1,0:T(4,128)S(1)} %get-tuple-element.594, f32[8,3,512]{2,1,0:T(4,128)S(1)} %get-tuple-element.595), kind=kLoop, calls=%fused_computation.55.clone.1 | loop fusion | flops 16777216 | bytes 8486912 | tf_op jit(solution)/shard_map/while/body/vmap()/reduce_sum | solution.py:82
  165.3 10.4 %fusion.76 = f32[8,9,512]{2,1,0:T(8,128)S(1)} fusion(f32[8,512,512]{2,1,0:T(8,128)} %multiply_reduce_fusion.2, f32[9,8,512]{2,0,1:T(8,128)S(1)} %stack.26), kind=kOutput, calls=%fused_computation.58.clone.1 | convolution fusion | flops 232783872 | bytes 8683520 | tf_op jit(solution)/shard_map/while/body/vmap()/dot_general | solution.py:84
  176.0 1.0 scatter_custom_fusion.6
  180.4 7.1 %multiply_reduce_fusion.2 = f32[8,512,512]{2,1,0:T(8,128)} fusion(f32[8,3,512]{2,1,0:T(4,128)S(1)} %get-tuple-element.594, f32[8,3,512]{2,1,0:T(4,128)S(1)} %get-tuple-element.595), kind=kLoop, calls=%fused_computation.55.clone.1 | loop fusion | flops 16777216 | bytes 8486912 | tf_op jit(solution)/shard_map/while/body/vmap()/reduce_sum | solution.py:82
  189.3 10.4 %fusion.76 = f32[8,9,512]{2,1,0:T(8,128)S(1)} fusion(f32[8,512,512]{2,1,0:T(8,128)} %multiply_reduce_fusion.2, f32[9,8,512]{2,0,1:T(8,128)S(1)} %stack.26), kind=kOutput, calls=%fused_computation.58.clone.1 | convolution fusion | flops 232783872 | bytes 8683520 | tf_op jit(solution)/shard_map/while/body/vmap()/dot_general | solution.py:84
  200.0 1.0 scatter_custom_fusion.6
  204.3 7.1 %multiply_reduce_fusion.2 = f32[8,512,512]{2,1,0:T(8,128)} fusion(f32[8,3,512]{2,1,0:T(4,128)S(1)} %get-tuple-element.594, f32[8,3,512]{2,1,0:T(4,128)S(1)} %get-tuple-element.595), kind=kLoop, calls=%fused_computation.55.clone.1 | loop fusion | flops 16777216 | bytes 8486912 | tf_op jit(solution)/shard_map/while/body/vmap()/reduce_sum | solution.py:82
  213.3 10.4 %fusion.76 = f32[8,9,512]{2,1,0:T(8,128)S(1)} fusion(f32[8,512,512]{2,1,0:T(8,128)} %multiply_reduce_fusion.2, f32[9,8,512]{2,0,1:T(8,128)S(1)} %stack.26), kind=kOutput, calls=%fused_computation.58.clone.1 | convolution fusion | flops 232783872 | bytes 8683520 | tf_op jit(solution)/shard_map/while/body/vmap()/dot_general | solution.py:84
  223.9 1.0 scatter_custom_fusion.6
  228.3 7.1 %multiply_reduce_fusion.2 = f32[8,512,512]{2,1,0:T(8,128)} fusion(f32[8,3,512]{2,1,0:T(4,128)S(1)} %get-tuple-element.594, f32[8,3,512]{2,1,0:T(4,128)S(1)} %get-tuple-element.595), kind=kLoop, calls=%fused_computation.55.clone.1 | loop fusion | flops 16777216 | bytes 8486912 | tf_op jit(solution)/shard_map/while/body/vmap()/reduce_sum | solution.py:82
  237.2 10.4 %fusion.76 = f32[8,9,512]{2,1,0:T(8,128)S(1)} fusion(f32[8,512,512]{2,1,0:T(8,128)} %multiply_reduce_fusion.2, f32[9,8,512]{2,0,1:T(8,128)S(1)} %stack.26), kind=kOutput, calls=%fused_computation.58.clone.1 | convolution fusion | flops 232783872 | bytes 8683520 | tf_op jit(solution)/shard_map/while/body/vmap()/dot_general | solution.py:84
  247.9 1.0 scatter_custom_fusion.6
  252.3 7.1 %multiply_reduce_fusion.2 = f32[8,512,512]{2,1,0:T(8,128)} fusion(f32[8,3,512]{2,1,0:T(4,128)S(1)} %get-tuple-element.594, f32[8,3,512]{2,1,0:T(4,128)S(1)} %get-tuple-element.595), kind=kLoop, calls=%fused_computation.55.clone.1 | loop fusion | flops 16777216 | bytes 8486912 | tf_op jit(solution)/shard_map/while/body/vmap()/reduce_sum | solution.py:82
  261.2 10.4 %fusion.76 = f32[8,9,512]{2,1,0:T(8,128)S(1)} fusion(f32[8,512,512]{2,1,0:T(8,128)} %multiply_reduce_fusion.2, f32[9,8,512]{2,0,1:T(8,128)S(1)} %stack.26), kind=kOutput, calls=%fused_computation.58.clone.1 | convolution fusion | flops 232783872 | bytes 8683520 | tf_op jit(solution)/shard_map/while/body/vmap()/dot_general | solution.py:84
  271.9 1.0 scatter_custom_fusion.6
  276.2 7.1 %multiply_reduce_fusion.2 = f32[8,512,512]{2,1,0:T(8,128)} fusion(f32[8,3,512]{2,1,0:T(4,128)S(1)} %get-tuple-element.594, f32[8,3,512]{2,1,0:T(4,128)S(1)} %get-tuple-element.595), kind=kLoop, calls=%fused_computation.55.clone.1 | loop fusion | flops 16777216 | bytes 8486912 | tf_op jit(solution)/shard_map/while/body/vmap()/reduce_sum | solution.py:82
  285.2 10.4 %fusion.76 = f32[8,9,512]{2,1,0:T(8,128)S(1)} fusion(f32[8,512,512]{2,1,0:T(8,128)} %multiply_reduce_fusion.2, f32[9,8,512]{2,0,1:T(8,128)S(1)} %stack.26), kind=kOutput, calls=%fused_computation.58.clone.1 | convolution fusion | flops 232783872 | bytes 8683520 | tf_op jit(solution)/shard_map/while/body/vmap()/dot_general | solution.py:84
  295.8 1.0 scatter_custom_fusion.6
  300.2 7.1 %multiply_reduce_fusion.2 = f32[8,512,512]{2,1,0:T(8,128)} fusion(f32[8,3,512]{2,1,0:T(4,128)S(1)} %get-tuple-element.594, f32[8,3,512]{2,1,0:T(4,128)S(1)} %get-tuple-element.595), kind=kLoop, calls=%fused_computation.55.clone.1 | loop fusion | flops 16777216 | bytes 8486912 | tf_op jit(solution)/shard_map/while/body/vmap()/reduce_sum | solution.py:82
  309.1 10.4 %fusion.76 = f32[8,9,512]{2,1,0:T(8,128)S(1)} fusion(f32[8,512,512]{2,1,0:T(8,128)} %multiply_reduce_fusion.2, f32[9,8,512]{2,0,1:T(8,128)S(1)} %stack.26), kind=kOutput, calls=%fused_computation.58.clone.1 | convolution fusion | flops 232783872 | bytes 8683520 | tf_op jit(solution)/shard_map/while/body/vmap()/dot_general | solution.py:84
  319.8 1.0 scatter_custom_fusion.6
  324.2 7.1 %multiply_reduce_fusion.2 = f32[8,512,512]{2,1,0:T(8,128)} fusion(f32[8,3,512]{2,1,0:T(4,128)S(1)} %get-tuple-element.594, f32[8,3,512]{2,1,0:T(4,128)S(1)} %get-tuple-element.595), kind=kLoop, calls=%fused_computation.55.clone.1 | loop fusion | flops 16777216 | bytes 8486912 | tf_op jit(solution)/shard_map/while/body/vmap()/reduce_sum | solution.py:82
  333.1 10.4 %fusion.76 = f32[8,9,512]{2,1,0:T(8,128)S(1)} fusion(f32[8,512,512]{2,1,0:T(8,128)} %multiply_reduce_fusion.2, f32[9,8,512]{2,0,1:T(8,128)S(1)} %stack.26), kind=kOutput, calls=%fused_computation.58.clone.1 | convolution fusion | flops 232783872 | bytes 8683520 | tf_op jit(solution)/shard_map/while/body/vmap()/dot_general | solution.py:84
  343.8 1.0 scatter_custom_fusion.6
  348.1 7.1 %multiply_reduce_fusion.2 = f32[8,512,512]{2,1,0:T(8,128)} fusion(f32[8,3,512]{2,1,0:T(4,128)S(1)} %get-tuple-element.594, f32[8,3,512]{2,1,0:T(4,128)S(1)} %get-tuple-element.595), kind=kLoop, calls=%fused_computation.55.clone.1 | loop fusion | flops 16777216 | bytes 8486912 | tf_op jit(solution)/shard_map/while/body/vmap()/reduce_sum | solution.py:82
  357.1 10.4 %fusion.76 = f32[8,9,512]{2,1,0:T(8,128)S(1)} fusion(f32[8,512,512]{2,1,0:T(8,128)} %multiply_reduce_fusion.2, f32[9,8,512]{2,0,1:T(8,128)S(1)} %stack.26), kind=kOutput, calls=%fused_computation.58.clone.1 | convolution fusion | flops 232783872 | bytes 8683520 | tf_op jit(solution)/shard_map/while/body/vmap()/dot_general | solution.py:84
  367.7 1.0 scatter_custom_fusion.6
  372.1 7.1 %multiply_reduce_fusion.2 = f32[8,512,512]{2,1,0:T(8,128)} fusion(f32[8,3,512]{2,1,0:T(4,128)S(1)} %get-tuple-element.594, f32[8,3,512]{2,1,0:T(4,128)S(1)} %get-tuple-element.595), kind=kLoop, calls=%fused_computation.55.clone.1 | loop fusion | flops 16777216 | bytes 8486912 | tf_op jit(solution)/shard_map/while/body/vmap()/reduce_sum | solution.py:82
  381.0 10.4 %fusion.76 = f32[8,9,512]{2,1,0:T(8,128)S(1)} fusion(f32[8,512,512]{2,1,0:T(8,128)} %multiply_reduce_fusion.2, f32[9,8,512]{2,0,1:T(8,128)S(1)} %stack.26), kind=kOutput, calls=%fused_computation.58.clone.1 | convolution fusion | flops 232783872 | bytes 8683520 | tf_op jit(solution)/shard_map/while/body/vmap()/dot_general | solution.py:84
  391.7 1.0 scatter_custom_fusion.6
  396.0 7.1 %multiply_reduce_fusion.2 = f32[8,512,512]{2,1,0:T(8,128)} fusion(f32[8,3,512]{2,1,0:T(4,128)S(1)} %get-tuple-element.594, f32[8,3,512]{2,1,0:T(4,128)S(1)} %get-tuple-element.595), kind=kLoop, calls=%fused_computation.55.clone.1 | loop fusion | flops 16777216 | bytes 8486912 | tf_op jit(solution)/shard_map/while/body/vmap()/reduce_sum | solution.py:82
  405.0 10.4 %fusion.76 = f32[8,9,512]{2,1,0:T(8,128)S(1)} fusion(f32[8,512,512]{2,1,0:T(8,128)} %multiply_reduce_fusion.2, f32[9,8,512]{2,0,1:T(8,128)S(1)} %stack.26), kind=kOutput, calls=%fused_computation.58.clone.1 | convolution fusion | flops 232783872 | bytes 8683520 | tf_op jit(solution)/shard_map/while/body/vmap()/dot_general | solution.py:84
  415.7 1.0 scatter_custom_fusion.6
  420.0 7.1 %multiply_reduce_fusion.2 = f32[8,512,512]{2,1,0:T(8,128)} fusion(f32[8,3,512]{2,1,0:T(4,128)S(1)} %get-tuple-element.594, f32[8,3,512]{2,1,0:T(4,128)S(1)} %get-tuple-element.595), kind=kLoop, calls=%fused_computation.55.clone.1 | loop fusion | flops 16777216 | bytes 8486912 | tf_op jit(solution)/shard_map/while/body/vmap()/reduce_sum | solution.py:82
  428.9 10.4 %fusion.76 = f32[8,9,512]{2,1,0:T(8,128)S(1)} fusion(f32[8,512,512]{2,1,0:T(8,128)} %multiply_reduce_fusion.2, f32[9,8,512]{2,0,1:T(8,128)S(1)} %stack.26), kind=kOutput, calls=%fused_computation.58.clone.1 | convolution fusion | flops 232783872 | bytes 8683520 | tf_op jit(solution)/shard_map/while/body/vmap()/dot_general | solution.py:84
  439.6 1.0 scatter_custom_fusion.6
  444.0 7.1 %multiply_reduce_fusion.2 = f32[8,512,512]{2,1,0:T(8,128)} fusion(f32[8,3,512]{2,1,0:T(4,128)S(1)} %get-tuple-element.594, f32[8,3,512]{2,1,0:T(4,128)S(1)} %get-tuple-element.595), kind=kLoop, calls=%fused_computation.55.clone.1 | loop fusion | flops 16777216 | bytes 8486912 | tf_op jit(solution)/shard_map/while/body/vmap()/reduce_sum | solution.py:82
  452.9 10.4 %fusion.76 = f32[8,9,512]{2,1,0:T(8,128)S(1)} fusion(f32[8,512,512]{2,1,0:T(8,128)} %multiply_reduce_fusion.2, f32[9,8,512]{2,0,1:T(8,128)S(1)} %stack.26), kind=kOutput, calls=%fused_computation.58.clone.1 | convolution fusion | flops 232783872 | bytes 8683520 | tf_op jit(solution)/shard_map/while/body/vmap()/dot_general | solution.py:84
  463.6 1.0 scatter_custom_fusion.6
  467.9 7.1 %multiply_reduce_fusion.2 = f32[8,512,512]{2,1,0:T(8,128)} fusion(f32[8,3,512]{2,1,0:T(4,128)S(1)} %get-tuple-element.594, f32[8,3,512]{2,1,0:T(4,128)S(1)} %get-tuple-element.595), kind=kLoop, calls=%fused_computation.55.clone.1 | loop fusion | flops 16777216 | bytes 8486912 | tf_op jit(solution)/shard_map/while/body/vmap()/reduce_sum | solution.py:82
  476.9 10.4 %fusion.76 = f32[8,9,512]{2,1,0:T(8,128)S(1)} fusion(f32[8,512,512]{2,1,0:T(8,128)} %multiply_reduce_fusion.2, f32[9,8,512]{2,0,1:T(8,128)S(1)} %stack.26), kind=kOutput, calls=%fused_computation.58.clone.1 | convolution fusion | flops 232783872 | bytes 8683520 | tf_op jit(solution)/shard_map/while/body/vmap()/dot_general | solution.py:84
  487.5 1.0 scatter_custom_fusion.6
  488.6 1.4 all_to_all.29
  490.0 9.7 %all-to-all-start.3 = ((f32[128,1,1536]{2,1,0:T(1,128)}), f32[128,1,1536]{2,1,0:T(1,128)S(1)}, u32[]{:S(2)}, u32[]{:S(2)}) async-start(f32[128,1,1536]{2,1,0:T(1,128)} %all_to_all.29), calls=%async_computation.3 | async-start | bytes 1572864 | tf_op jit(solution)/shard_map/all_to_all | solution.py:157
  499.7 2.4 reduce
  502.1 14.1 %all-to-all-done.3 = f32[128,1,1536]{2,1,0:T(1,128)S(1)} async-done(((f32[128,1,1536]{2,1,0:T(1,128)}), f32[128,1,1536]{2,1,0:T(1,128)S(1)}, u32[]{:S(2)}, u32[]{:S(2)}) %all-to-all-start.3) | async-done | bytes 786464 | tf_op jit(solution)/shard_map/all_to_all | solution.py:157
  517.2 41.6 %while.38 = (s32[]{:T(128)}, f32[16,3,1024]{2,1,0:T(4,128)S(1)}, f32[16,3,512]{2,0,1:T(8,128)S(1)}, f32[16,3,1024]{2,1,0:T(4,128)}, s32[]{:T(128)}, /*index=5*/s32[]{:T(128)}, s32[]{}, s32[]{}) while((s32[]{:T(128)}, f32[16,3,1024]{2,1,0:T(4,128)S(1)}, f32[16,3,512]{2,0,1:T(8,128)S(1)}, f32[16,3,1024]{2,1,0:T(4,128)}, ...), condition=%wide.region_20.23_spmd.clone.clone, body=%wide.region_14.22_spmd.clone.clone.sunk | while | flops 19748164 | bytes 1173953 | solution.py:165
  (946 shorter events, 183.0 us)
Async XLA Ops:
  0.0 85.3 %copy-start.2 = (s32[1,128]{1,0:T(1,128)S(1)}, s32[1,128]{1,0:T(1,128)}, u32[]{:S(2)}) copy-start(s32[1,128]{1,0:T(1,128)} %param.22) | copy-start | bytes 1540
  0.0 85.2 %copy-start.3 = (s32[1,128]{1,0:T(1,128)S(1)}, s32[1,128]{1,0:T(1,128)}, u32[]{:S(2)}) copy-start(s32[1,128]{1,0:T(1,128)} %param.21) | copy-start | bytes 1540
  0.0 84.1 %copy-start.1 = (f32[3,2048]{1,0:T(4,128)S(1)}, f32[3,2048]{1,0:T(4,128)}, u32[]{:S(2)}) copy-start(f32[3,2048]{1,0:T(4,128)} %param.19) | copy-start | bytes 73732
  0.0 105.0 %copy-start = (f32[2048]{0:T(1024)S(1)}, f32[2048]{0:T(1024)}, u32[]{:S(2)}) copy-start(f32[2048]{0:T(1024)} %param.20) | copy-start | bytes 24580
  4.7 65.1 %all-to-all-start.1 = ((s32[128,1,1]{2,1,0:T(1,128)}), s32[128,1,1]{2,1,0:T(1,128)S(1)}, u32[]{:S(2)}, u32[]{:S(2)}) async-start(s32[128,1,1]{2,1,0:T(1,128)} %copy.31), calls=%async_computation.1 | async-start | bytes 131072 | tf_op jit(solution)/shard_map/all_to_all | solution.py:127
  74.3 26.3 %all-to-all-start.2 = ((f32[128,1,1536]{2,1,0:T(1,128)}), f32[128,1,1536]{2,1,0:T(1,128)S(1)}, u32[]{:S(2)}, u32[]{:S(2)}) async-start(f32[128,1,1536]{2,1,0:T(1,128)} %copy.32), calls=%async_computation.2 | async-start | bytes 1572864 | tf_op jit(solution)/shard_map/all_to_all | solution.py:132
  100.6 389.5 %all-to-all-start = ((s32[128,1,1]{2,1,0:T(1,128)}), s32[128,1,1]{2,1,0:T(1,128)S(1)}, u32[]{:S(2)}, u32[]{:S(2)}) async-start(s32[128,1,1]{2,1,0:T(1,128)} %copy.30), calls=%async_computation | async-start | bytes 131072 | tf_op jit(solution)/shard_map/all_to_all | solution.py:158
  490.0 26.2 %all-to-all-start.3 = ((f32[128,1,1536]{2,1,0:T(1,128)}), f32[128,1,1536]{2,1,0:T(1,128)S(1)}, u32[]{:S(2)}, u32[]{:S(2)}) async-start(f32[128,1,1536]{2,1,0:T(1,128)} %all_to_all.29), calls=%async_computation.3 | async-start | bytes 1572864 | tf_op jit(solution)/shard_map/all_to_all | solution.py:157
  558.9 0.7 copy-start.4
where the time goes:
time: 565 us; the launch traced here: 560 us
  matrix products  195 us (35%)
  other arithmetic  187 us (33%)
  local copies, waits for them, and re-layouts  109 us (19%)
  starting transfers between devices  35.2 us (6%)
  waiting for transfers between devices  29.4 us (5%)
    dot_general x16, matrix products, tile_from_features(): jnp.dot(feature_rows, kernel, precision=lax.Precision.HIGHEST, preferred_...  166 us
    reduce_sum x16, other arithmetic, tile_from_features(): radius_sq = jnp.sum(offset * offset, axis=0) + smoothing_sq  114 us
    slice x32, local copies, waits for them, and re-layouts, basis_parts(): basis_y = lagrange(coords[1], cheb_nodes)  27.2 us
    scatter-add x16, other arithmetic, add_group(): outgoing.at[group_target_slots]  16.6 us
    all_to_all x1, waiting for transfers between devices, local(): lax.all_to_all(answer, ('gx', 'gy'), split_axis=0, concat_axis=0, tiled=T...  15.3 us
    dot_general x16, matrix products, upward(): jnp.einsum('ai,cei->cae', basis_x, weighted, precision=lax.Precision.HIGH...  14.4 us
    all_to_all x1, waiting for transfers between devices, local(): lax.all_to_all(outgoing, ('gx', 'gy'), split_axis=0, concat_axis=0, tiled...  14.1 us
    dot_general x16, matrix products, downward(): jnp.einsum('cae,ai->cei', shaped, basis_x, precision=lax.Precision.HIGHEST)  14 us
  transfers between devices with their start and end apart: 4, of which 2 were waited for; matrix products, arithmetic and copies ran while one was open for 78% of the time, Pallas kernels for 0%

commit v1 on v0

v1 whole, which is shorter than its diff:
```python
import functools
import math

import jax
import jax.numpy as jnp
import numpy as np
from jax import lax
from jax.experimental import pallas as pl
from jax.experimental.pallas import tpu as pltpu
from jax.sharding import PartitionSpec as P

CL_DEV = 16
PTS = 1024
DEG = 7
TILES_DEV = 128
DOMAINS = 128
NODES = DEG + 1
AXES = ("gx", "gy")

smoothing_sq = 0.01
biot_factor = -0.07957747154594767

node_values = np.cos(np.pi * np.arange(NODES) / DEG)
node_list = [float(v) for v in node_values.astype(np.float32)]
node_scales = [
    1.0 / math.prod(node_list[a] - node_list[m] for m in range(NODES) if m != a)
    for a in range(NODES)
]


def build_constants():
    nodes = node_values.astype(np.float32)
    lane = np.arange(128)
    table = np.zeros((8, 8, 128), np.float32)
    for group in range(4):
        table[group] = nodes[group + 4 * (lane // 64)][None, :]
    table[4] = nodes[(lane // 8) % 8][None, :]
    table[5] = nodes[lane % 8][None, :]
    table[6] = nodes[:, None]
    table[7, :4] = table[:4, 0]
    return table


CONSTANTS = build_constants()


def split_bf16(value):
    high = value.astype(jnp.bfloat16)
    return high, (value - high.astype(jnp.float32)).astype(jnp.bfloat16)


def lagrange_rows(row, sublane):
    spread = jnp.broadcast_to(row, (NODES, row.shape[1]))
    result = None
    for m in range(NODES):
        factor = jnp.where(sublane == m, node_scales[m], spread - node_list[m])
        result = factor if result is None else result * factor
    return result


def paired_rows(basis_y, basis_z):
    return jnp.concatenate([basis_y[b : b + 1] * basis_z for b in range(NODES)], axis=0)


def upward_kernel(width_ref, coord_ref, strength_ref, const_ref, feature_ref, basis_ref, rows_ref):
    sublane = lax.broadcasted_iota(jnp.int32, (NODES, PTS), 0)
    lane = lax.broadcasted_iota(jnp.int32, (8, 128), 1)

    @pl.loop(0, CL_DEV)
    def _(cluster):
        start = pl.multiple_of(cluster * PTS, PTS)
        where = pl.ds(start, PTS)
        basis = [lagrange_rows(coord_ref[axis : axis + 1, where], sublane) for axis in range(3)]
        for axis in range(3):
            basis_ref[8 * axis : 8 * axis + 8, where] = basis[axis]
        paired = paired_rows(basis[1], basis[2])
        weighted = jnp.concatenate(
            [strength_ref[c : c + 1, where] * basis[0] for c in range(3)], axis=0
        )
        paired_high, paired_low = split_bf16(paired)
        weighted_high, weighted_low = split_bf16(weighted)
        left = jnp.concatenate([weighted_high, weighted_low], axis=0)
        contract = functools.partial(
            lax.dot_general,
            dimension_numbers=(((1,), (1,)), ((), ())),
            preferred_element_type=jnp.float32,
        )
        twice_high = jnp.concatenate([paired_high, paired_high], axis=0)
        twice_low = jnp.concatenate([paired_low, paired_low], axis=0)
        by_high = contract(left, twice_high)
        by_low = contract(weighted_high, twice_low)
        charge = by_high[:24] + by_high[24:] + by_low
        charge = charge * biot_factor
        charges = []
        for c in range(3):
            block = charge[8 * c : 8 * c + 8]
            moved = jnp.concatenate([block[4:], block[:4]], axis=0)
            charges.append(jnp.where(lane < 64, block, moved))
        width = width_ref[cluster]
        node_x = const_ref[7] * width
        node_y = const_ref[4] * width
        node_z = const_ref[5] * width
        moments = [
            node_y * charges[2] - node_z * charges[1],
            node_z * charges[0] - node_x * charges[2],
            node_x * charges[1] - node_y * charges[0],
        ]
        order = [charges[0], charges[1], charges[2], charges[0], charges[1]] + moments
        for row, value in enumerate(order):
            for group in range(4):
                rows_ref[row : row + 1, 128 * group : 128 * group + 128] = value[group : group + 1]
        high, low = split_bf16(rows_ref[...])
        feature_ref[cluster] = jnp.concatenate([high, low], axis=0)


def tile_kernel(domain_ref, request_ref, center_ref, width_ref, feature_ref, const_ref, out_ref, order_ref, high_ref, low_ref):
    sublane = lax.broadcasted_iota(jnp.int32, (8, 128), 0)

    def collect(peer, count):
        order_ref[count] = peer
        return count + (request_ref[peer, 0, 0] > 0).astype(jnp.int32)

    total = lax.fori_loop(0, DOMAINS, collect, 0)
    domain = domain_ref[0]

    @pl.loop(0, total)
    def _(step):
        peer = order_ref[step]
        local_id = request_ref[peer, 0, 0] - 1
        source = domain * CL_DEV + local_id
        target = request_ref[peer, 0, 1]
        source_width = width_ref[source]
        target_width = width_ref[target]
        shift = [center_ref[axis, target] - center_ref[axis, source] for axis in range(3)]
        target_x = [const_ref[group] * target_width + shift[0] for group in range(4)]
        target_y = const_ref[4] * target_width + shift[1]
        target_z = const_ref[5] * target_width + shift[2]
        apart_z = target_z - const_ref[6] * source_width
        square_z = apart_z * apart_z + smoothing_sq
        square_yz = []
        for b in range(NODES):
            apart_y = target_y - source_width * node_list[b]
            square_yz.append(square_z + apart_y * apart_y)
        for group in range(4):
            for half in range(2):
                source_x = source_width * node_list[group + 4 * half]
                for lanes in range(4):
                    apart_x = target_x[lanes] - source_x
                    square_x = apart_x * apart_x
                    for b in range(0, NODES, 2):
                        pair = []
                        for part in range(2):
                            inverse = lax.rsqrt(square_yz[b + part] + square_x)
                            pair.append(inverse * inverse * inverse)
                        kernel = jnp.concatenate(pair, axis=0)
                        high, low = split_bf16(kernel)
                        first = group * 128 + half * 64 + b * 8
                        place = (slice(first, first + 16), slice(128 * lanes, 128 * lanes + 128))
                        high_ref[place] = high
                        low_ref[place] = low
        feature = feature_ref[local_id]
        summed = jnp.dot(feature, high_ref[...], preferred_element_type=jnp.float32)
        summed += jnp.dot(feature, low_ref[...], preferred_element_type=jnp.float32)
        summed = summed[:8] + summed[8:]
        for lanes in range(4):
            block = summed[:, 128 * lanes : 128 * lanes + 128]
            first = jnp.where(sublane == 0, target_y, jnp.where(sublane == 1, target_z, target_x[lanes]))
            second = jnp.where(sublane == 0, target_z, jnp.where(sublane == 1, target_x[lanes], target_y))
            velocity = (
                first * pltpu.roll(block, 6, 0)
                - second * pltpu.roll(block, 7, 0)
                - pltpu.roll(block, 3, 0)
            )
            for c in range(3):
                out_ref[peer * 12 + c * 4 + lanes] = velocity[c : c + 1]


def relay_kernel(order_ref, in_ref, out_ref):
    @pl.loop(0, DOMAINS, step=4)
    def _(first):
        for extra in range(4):
            peer = first + extra
            place = order_ref[peer]
            rows = in_ref[pl.ds(jnp.maximum(place, 0) * 12, 12)]
            out_ref[pl.ds(peer * 12, 12)] = jnp.where(place < 0, 0.0, rows)


def downward_kernel(owner_ref, part_ref, basis_ref, out_ref, proxy_ref):
    cluster_row = lax.broadcasted_iota(jnp.int32, (CL_DEV, DOMAINS), 0)
    assign = (owner_ref[...] == cluster_row + 1).astype(jnp.bfloat16)
    for chunk in range(12):
        high, low = split_bf16(part_ref[pl.ds(chunk, DOMAINS, stride=12), :])
        proxy_ref[chunk * CL_DEV : (chunk + 1) * CL_DEV] = jnp.dot(
            assign, high, preferred_element_type=jnp.float32
        ) + jnp.dot(assign, low, preferred_element_type=jnp.float32)

    @pl.loop(0, CL_DEV)
    def _(cluster):
        start = pl.multiple_of(cluster * PTS, PTS)
        where = pl.ds(start, PTS)
        rows = proxy_ref[pl.ds(cluster, 12, stride=CL_DEV), :]
        near, far = rows[:, :64], rows[:, 64:]
        left = jnp.concatenate(
            [piece[4 * c : 4 * c + 4] for c in range(3) for piece in (near, far)], axis=0
        )
        left_high, left_low = split_bf16(left)
        paired = paired_rows(basis_ref[8:16, where], basis_ref[16:24, where])
        paired_high, paired_low = split_bf16(paired)
        spread = jnp.dot(
            jnp.concatenate([left_high, left_low], axis=0),
            paired_high,
            preferred_element_type=jnp.float32,
        )
        spread = spread[:24] + spread[24:] + jnp.dot(
            left_high, paired_low, preferred_element_type=jnp.float32
        )
        basis_x = basis_ref[0:8, where]
        for c in range(3):
            out_ref[c : c + 1, where] = jnp.sum(
                spread[8 * c : 8 * c + 8] * basis_x, axis=0, keepdims=True
            )


def in_vmem():
    return pl.BlockSpec(memory_space=pltpu.VMEM)


def in_smem():
    return pl.BlockSpec(memory_space=pltpu.SMEM)


def exchange(value):
    return lax.all_to_all(value, AXES, split_axis=0, concat_axis=0, tiled=True)


def local(point_coords, strengths, centers, half_widths, tile_source, tile_target, tile_count):
    domain = lax.axis_index(AXES)
    const = jnp.asarray(CONSTANTS)
    source_ids = tile_source[0]
    target_ids = tile_target[0]
    alive = jnp.arange(TILES_DEV) < tile_count[0]
    slots = jnp.arange(DOMAINS)[:, None]
    from_source = (slots == (source_ids // CL_DEV)[None, :]) & alive[None, :]
    from_target = (slots == (target_ids // CL_DEV)[None, :]) & alive[None, :]
    source_code = jnp.sum(
        jnp.where(from_source, (target_ids * 32 + source_ids % CL_DEV + 1)[None, :], 0), axis=1
    )
    target_code = jnp.sum(
        jnp.where(
            from_target, ((source_ids // CL_DEV) * 32 + target_ids % CL_DEV + 1)[None, :], 0
        ),
        axis=1,
    )
    message = jnp.stack([source_code % 32, source_code // 32, target_code % 32], axis=1)
    relay_order = jnp.where(target_code > 0, target_code // 32, -1)
    received = exchange(message.reshape(DOMAINS, 1, 3))

    own_widths = lax.dynamic_slice_in_dim(half_widths, domain * CL_DEV, CL_DEV)
    features, basis = pl.pallas_call(
        upward_kernel,
        out_shape=(
            jax.ShapeDtypeStruct((CL_DEV, 16, 512), jnp.bfloat16),
            jax.ShapeDtypeStruct((24, CL_DEV * PTS), jnp.float32),
        ),
        in_specs=[in_smem(), in_vmem(), in_vmem(), in_vmem()],
        out_specs=(in_vmem(), in_vmem()),
        scratch_shapes=[pltpu.VMEM((8, 512), jnp.float32)],
        cost_estimate=pl.CostEstimate(flops=10**8, bytes_accessed=2 * 10**6, transcendentals=0),
        name="upward",
    )(own_widths, point_coords, strengths, const)

    parts = pl.pallas_call(
        tile_kernel,
        out_shape=jax.ShapeDtypeStruct((DOMAINS * 12, 1, 128), jnp.float32),
        in_specs=[in_smem(), in_smem(), in_smem(), in_smem(), in_vmem(), in_vmem()],
        out_specs=in_vmem(),
        scratch_shapes=[
            pltpu.SMEM((DOMAINS,), jnp.int32),
            pltpu.VMEM((512, 512), jnp.bfloat16),
            pltpu.VMEM((512, 512), jnp.bfloat16),
        ],
        name="tiles",
    )(domain.reshape(1), received, centers, half_widths, features, const)

    relayed = exchange(parts.reshape(DOMAINS, 1, 1536))
    ordered = pl.pallas_call(
        relay_kernel,
        out_shape=jax.ShapeDtypeStruct((DOMAINS * 12, 1, 128), jnp.float32),
        in_specs=[in_smem(), in_vmem()],
        out_specs=in_vmem(),
        name="relay",
    )(relay_order, relayed.reshape(DOMAINS * 12, 1, 128))
    arrived = exchange(ordered.reshape(DOMAINS, 1, 1536))

    owners = received[:, 0, 2]
    return pl.pallas_call(
        downward_kernel,
        out_shape=jax.ShapeDtypeStruct((3, CL_DEV * PTS), jnp.float32),
        in_specs=[in_vmem(), in_vmem(), in_vmem()],
        out_specs=in_vmem(),
        scratch_shapes=[pltpu.VMEM((12 * CL_DEV, 128), jnp.float32)],
        name="downward",
    )(owners.reshape(1, DOMAINS), arrived.reshape(DOMAINS * 12, 128), basis)


def solution(mesh):
    return jax.shard_map(
        local,
        mesh=mesh,
        in_specs=(
            P(None, AXES),
            P(None, AXES),
            P(),
            P(),
            P(AXES, None),
            P(AXES, None),
            P(AXES),
        ),
        out_specs=P(None, AXES),
        check_vma=False,
    )
```

time: 565 us -> 127 us (0.22)
  matrix products: 195 us -> 0 us
  other arithmetic: 187 us -> 1.35 us
  local copies, waits for them, and re-layouts: 109 us -> 7.56 us
  Pallas kernels: 0 us -> 55.4 us
    dot_general x50 -> x0, matrix products: 195 us -> none  [the longest x16 166 us: tile_from_features(): jnp.dot(feature_rows, kernel, precision=lax.Precision.HIGHEST, preferred_...]
    reduce_sum x19 -> x1, other arithmetic: 115 us -> 0.11 us  [local(): jnp.sum(jnp.where(from_source, (target_ids * 32 + source_ids % CL_DEV + 1...]
    pallas_call x0 -> x4, Pallas kernels: none -> 55.4 us  [the longest x1 37.9 us: local(): pl.pallas_call(tile_kernel, out_shape=jax.ShapeDtypeStruct((DOMAINS * 12,...]
    gather x96 -> x0, local copies, waits for them, and re-layouts: 48 us -> none  [the longest x16 10.2 us: add_group(): jnp.take(half_widths, group_targets)]
    slice x32 -> x1, local copies, waits for them, and re-layouts: 27.2 us -> 3.09 us  [local(): owners = received[:, 0, 2]]
    scatter-add x16 -> x0, other arithmetic: 16.6 us -> none  [add_group(): outgoing.at[group_target_slots]]
    reduce_prod x64 -> x0, other arithmetic: 15 us -> none  [the longest x32 9.16 us: lagrange(): jnp.prod(jnp.where(diagonal[:, :, None], 1.0, differ[None, :, :]), axis=1)]
    and x32 -> x0, other arithmetic: 12.9 us -> none  [the longest x16 11.6 us: add_group(): jnp.take(fetched, group_source_slots, axis=0)]
  transfers between devices with their start and end apart: 4 -> 3, of which waited for: 2 -> 3; matrix products, arithmetic and copies ran while one was open for 78% -> 4% of each run, Pallas kernels for 0% -> 6%
where the time goes in v1:
time: 127 us
  Pallas kernels  55.4 us (44%)
  starting transfers between devices  31.3 us (25%)
  waiting for transfers between devices  30.4 us (24%)
  local copies, waits for them, and re-layouts  7.56 us (6%)
  other arithmetic  1.35 us (1%)
    pallas_call x1, Pallas kernels, local(): pl.pallas_call(tile_kernel, out_shape=jax.ShapeDtypeStruct((DOMAINS * 12,...  37.9 us
    all_to_all x3, starting transfers between devices, exchange(): return lax.all_to_all(value, AXES, split_axis=0, concat_axis=0, tiled=True)  31.3 us
    all_to_all x3, waiting for transfers between devices, exchange(): return lax.all_to_all(value, AXES, split_axis=0, concat_axis=0, tiled=True)  30.4 us
    pallas_call x1, Pallas kernels, local(): pl.pallas_call(upward_kernel, out_shape=(jax.ShapeDtypeStruct((CL_DEV, 16...  7.34 us
    pallas_call x1, Pallas kernels, local(): pl.pallas_call(downward_kernel, out_shape=jax.ShapeDtypeStruct((3, CL_DEV...  6.99 us
    pallas_call x1, Pallas kernels, local(): pl.pallas_call(relay_kernel, out_shape=jax.ShapeDtypeStruct((DOMAINS * 12...  3.15 us
    slice x1, local copies, waits for them, and re-layouts, local(): owners = received[:, 0, 2]  3.09 us
  transfers between devices with their start and end apart: 3, of which 3 were waited for; matrix products, arithmetic and copies ran while one was open for 4% of the time, Pallas kernels for 6%

profile of v1, /device:TPU:1, one launch (start us, length us, event | category | flops | bytes accessed | tf_op | source)
XLA Modules:
  0.0 126.7 jit_solution(6381129229355629696)
XLA Ops:
  0.7 0.7 add_bitcast_fusion
  1.4 0.1 select_reduce_fusion.1
  1.5 0.7 copy.26
  2.2 11.5 %all-to-all-start = ((s32[128,1,3]{2,1,0:T(1,128)}), s32[128,1,3]{2,1,0:T(1,128)S(1)}, u32[]{:S(2)}, u32[]{:S(2)}) async-start(s32[128,1,3]{2,1,0:T(1,128)} %bitcast.7), calls=%async_computation | async-start | bytes 131072 | tf_op jit(solution)/shard_map/all_to_all | solution.py:233
  13.7 1.3 %dynamic_slice.3.width_ref = f32[16]{0:T(128)} dynamic-slice(f32[2048]{0:T(1024)} %width_ref.1, s32[]{:T(128)S(6)} %select_n.85), dynamic_slice_sizes={16} | dynamic-slice | bytes 132 | tf_op jit(solution)/shard_map/dynamic_slice | solution.py:258
  15.1 7.3 %upward.1 = (bf16[16,16,512]{2,1,0:T(8,128)(2,1)}, f32[24,16384]{1,0:T(8,128)}) custom-call(f32[16]{0:T(128)} %dynamic_slice.3.width_ref, f32[3,16384]{1,0:T(4,128)} %coord_ref.1, f32[3,16384]{1,0:T(4,128)} %strength_ref.1, f32[8,8,128]{2,1,0:T(8,128)} %constant.92.clone.const_ref), custom_call_target="tpu_custom_call" | custom-call | flops 100000000 | bytes 2000000 | tf_op jit(solution)/shard_map/upward/pallas_call | solution.py:259
  22.4 0.9 all-to-all-done.request_ref
  23.3 0.0 copy-start.2
  23.3 0.6 copy-done.2
  23.9 37.9 %tiles.1 = f32[1536,1,128]{2,1,0:T(1,128)} custom-call(s32[1]{0:T(128)} %bitcast.8.domain_ref, s32[128,1,3]{2,1,0:T(1,128)} %copy-done.2, f32[3,2048]{1,0:T(4,128)} %center_ref.1, f32[2048]{0:T(1024)} %width_ref.1, bf16[16,16,512]{2,1,0:T(8,128)(2,1)} %get-tuple-element.7.feature_ref, f32[8,8,128]{2,1,0:T(8,128)} %constant.92.clone.const_ref), custom_call_target="tpu_custom_call" | custom-call | tf_op jit(solution)/shard_map/tiles/pallas_call | solution.py:272
  61.8 15.6 %all-to-all-start.1 = ((f32[128,1,1536]{2,1,0:T(1,128)}), f32[128,1,1536]{2,1,0:T(1,128)S(1)}, u32[]{:S(2)}, u32[]{:S(2)}) async-start(f32[128,1,1536]{2,1,0:T(1,128)} %bitcast.34), calls=%async_computation.1 | async-start | bytes 1572864 | tf_op jit(solution)/shard_map/all_to_all | solution.py:233
  77.4 0.5 compare_select_fusion.2.order_ref
  77.9 16.0 %all-to-all-done.1 = f32[128,1,1536]{2,1,0:T(1,128)S(1)} async-done(((f32[128,1,1536]{2,1,0:T(1,128)}), f32[128,1,1536]{2,1,0:T(1,128)S(1)}, u32[]{:S(2)}, u32[]{:S(2)}) %all-to-all-start.1) | async-done | bytes 786464 | tf_op jit(solution)/shard_map/all_to_all | solution.py:233
  93.9 0.0 copy-start
  93.9 0.9 copy-done
  94.8 0.0 copy-start.3
  94.8 3.1 %relay.1 = f32[1536,1,128]{2,1,0:T(1,128)} custom-call(s32[128]{0:T(128)} %compare_select_fusion.2.order_ref, f32[1536,1,128]{2,1,0:T(1,128)} %bitcast.33), custom_call_target="tpu_custom_call" | custom-call | tf_op jit(solution)/shard_map/relay/pallas_call | solution.py:286
  97.9 4.3 %all-to-all-start.2 = ((f32[128,1,1536]{2,1,0:T(1,128)}), f32[128,1,1536]{2,1,0:T(1,128)S(1)}, u32[]{:S(2)}, u32[]{:S(2)}) async-start(f32[128,1,1536]{2,1,0:T(1,128)} %bitcast.35), calls=%async_computation.2 | async-start | bytes 1572864 | tf_op jit(solution)/shard_map/all_to_all | solution.py:233
  102.2 0.0 copy-done.3
  102.2 3.1 %slice_reduce_fusion = s32[128]{0:T(128)} fusion(s32[128,1,3]{2,1,0:T(1,128)S(1)} %copy-done.3), kind=kLoop, calls=%fused_computation | loop fusion | bytes 1024 | tf_op jit(solution)/shard_map/slice | solution.py:295
  105.3 13.5 %all-to-all-done.2 = f32[128,1,1536]{2,1,0:T(1,128)S(1)} async-done(((f32[128,1,1536]{2,1,0:T(1,128)}), f32[128,1,1536]{2,1,0:T(1,128)S(1)}, u32[]{:S(2)}, u32[]{:S(2)}) %all-to-all-start.2) | async-done | bytes 786464 | tf_op jit(solution)/shard_map/all_to_all | solution.py:233
  118.9 0.0 copy-start.1
  118.9 0.9 copy-done.1
  119.8 7.0 %downward.1 = f32[3,16384]{1,0:T(4,128)} custom-call(s32[1,128]{1,0:T(1,128)} %bitcast.38, f32[1536,128]{1,0:T(8,128)} %bitcast.36, f32[24,16384]{1,0:T(8,128)} %get-tuple-element.8.basis_ref), custom_call_target="tpu_custom_call" | custom-call | tf_op jit(solution)/shard_map/downward/pallas_call | solution.py:296
  (3 shorter events, 0.0 us)
Async XLA Ops:
  2.2 21.1 %all-to-all-start = ((s32[128,1,3]{2,1,0:T(1,128)}), s32[128,1,3]{2,1,0:T(1,128)S(1)}, u32[]{:S(2)}, u32[]{:S(2)}) async-start(s32[128,1,3]{2,1,0:T(1,128)} %bitcast.7), calls=%async_computation | async-start | bytes 131072 | tf_op jit(solution)/shard_map/all_to_all | solution.py:233
  23.3 0.6 copy-start.2
  61.8 32.1 %all-to-all-start.1 = ((f32[128,1,1536]{2,1,0:T(1,128)}), f32[128,1,1536]{2,1,0:T(1,128)S(1)}, u32[]{:S(2)}, u32[]{:S(2)}) async-start(f32[128,1,1536]{2,1,0:T(1,128)} %bitcast.34), calls=%async_computation.1 | async-start | bytes 1572864 | tf_op jit(solution)/shard_map/all_to_all | solution.py:233
  93.9 0.9 copy-start
  94.8 7.5 %copy-start.3 = (s32[128,1,3]{2,1,0:T(1,128)S(1)}, s32[128,1,3]{2,1,0:T(1,128)}, u32[]{:S(2)}) copy-start(s32[128,1,3]{2,1,0:T(1,128)} %copy-done.2) | copy-start | bytes 4612
  97.9 20.9 %all-to-all-start.2 = ((f32[128,1,1536]{2,1,0:T(1,128)}), f32[128,1,1536]{2,1,0:T(1,128)S(1)}, u32[]{:S(2)}, u32[]{:S(2)}) async-start(f32[128,1,1536]{2,1,0:T(1,128)} %bitcast.35), calls=%async_computation.2 | async-start | bytes 1572864 | tf_op jit(solution)/shard_map/all_to_all | solution.py:233
  118.9 0.9 copy-start.1

commit v2 on v1

v2 whole, which is shorter than its diff:
```python
import functools
import math

import jax
import jax.numpy as jnp
import numpy as np
from jax import lax
from jax.experimental import pallas as pl
from jax.experimental.pallas import tpu as pltpu
from jax.sharding import PartitionSpec as P

CL_DEV = 16
PTS = 1024
DEG = 7
TILES_DEV = 128
DOMAINS = 128
NODES = DEG + 1
GROUP = 4
AXES = ("gx", "gy")

smoothing_sq = 0.01
biot_factor = -0.07957747154594767

node_values = np.cos(np.pi * np.arange(NODES) / DEG)
node_list = [float(v) for v in node_values.astype(np.float32)]
node_scales = [
    1.0 / math.prod(node_list[a] - node_list[m] for m in range(NODES) if m != a)
    for a in range(NODES)
]


def build_constants():
    nodes = node_values.astype(np.float32)
    lane = np.arange(128)
    table = np.zeros((8, 8, 128), np.float32)
    for group in range(4):
        table[group] = nodes[group + 4 * (lane // 64)][None, :]
    table[4] = nodes[(lane // 8) % 8][None, :]
    table[5] = nodes[lane % 8][None, :]
    table[6] = nodes[:, None]
    table[7, :4] = table[:4, 0]
    return table


CONSTANTS = build_constants()


def split_bf16(value):
    high = value.astype(jnp.bfloat16)
    return high, (value - high.astype(jnp.float32)).astype(jnp.bfloat16)


def lagrange_rows(row, sublane):
    spread = jnp.broadcast_to(row, (NODES, row.shape[1]))
    result = None
    for m in range(NODES):
        factor = jnp.where(sublane == m, node_scales[m], spread - node_list[m])
        result = factor if result is None else result * factor
    return result


def paired_rows(basis_y, basis_z):
    return jnp.concatenate([basis_y[b : b + 1] * basis_z for b in range(NODES)], axis=0)


def message_kernel(count_ref, source_ref, target_ref, out_ref):
    slot = lax.broadcasted_iota(jnp.int32, (DOMAINS, TILES_DEV), 0)
    lane = lax.broadcasted_iota(jnp.int32, (DOMAINS, TILES_DEV), 1)
    alive = lane < count_ref[0]
    source = source_ref[...]
    target = target_ref[...]
    from_source = (slot == source // CL_DEV) & alive
    from_target = (slot == target // CL_DEV) & alive
    source_code = jnp.sum(
        jnp.where(from_source, target * 32 + source % CL_DEV + 1, 0), axis=1, keepdims=True
    )
    target_local = jnp.sum(
        jnp.where(from_target, target % CL_DEV + 1, 0), axis=1, keepdims=True
    )
    out_ref[...] = jnp.where(
        lane == 0,
        source_code % 32,
        jnp.where(lane == 1, source_code // 32, jnp.where(lane == 2, target_local, 0)),
    )


def basis_kernel(coord_ref, basis_ref):
    sublane = lax.broadcasted_iota(jnp.int32, (NODES, PTS), 0)

    @pl.loop(0, CL_DEV)
    def _(cluster):
        where = pl.ds(pl.multiple_of(cluster * PTS, PTS), PTS)
        for axis in range(3):
            basis_ref[8 * axis : 8 * axis + 8, where] = lagrange_rows(
                coord_ref[axis : axis + 1, where], sublane
            )


def upward_kernel(domain_ref, width_ref, coord_ref, strength_ref, const_ref, center_ref, all_width_ref, feature_ref, place_ref, same_ref, rows_ref):
    same_ref[...] = const_ref[...]
    place_ref[0:3] = center_ref[...]
    place_ref[3:4] = all_width_ref[...]
    sublane = lax.broadcasted_iota(jnp.int32, (NODES, PTS), 0)
    lane = lax.broadcasted_iota(jnp.int32, (8, 128), 1)

    def one_cluster(cluster, rows):
        where = pl.ds(pl.multiple_of(cluster * PTS, PTS), PTS)
        basis = [lagrange_rows(coord_ref[axis : axis + 1, where], sublane) for axis in range(3)]
        paired = paired_rows(basis[1], basis[2])
        weighted = jnp.concatenate(
            [strength_ref[c : c + 1, where] * basis[0] for c in range(3)], axis=0
        )
        paired_high, paired_low = split_bf16(paired)
        weighted_high, weighted_low = split_bf16(weighted)
        left = jnp.concatenate([weighted_high, weighted_low], axis=0)
        contract = functools.partial(
            lax.dot_general,
            dimension_numbers=(((1,), (1,)), ((), ())),
            preferred_element_type=jnp.float32,
        )
        twice_high = jnp.concatenate([paired_high, paired_high], axis=0)
        twice_low = jnp.concatenate([paired_low, paired_low], axis=0)
        by_high = contract(left, twice_high)
        by_low = contract(weighted_high, twice_low)
        charge = by_high[:24] + by_high[24:] + by_low
        charge = charge * biot_factor
        charges = []
        for c in range(3):
            block = charge[8 * c : 8 * c + 8]
            moved = jnp.concatenate([block[4:], block[:4]], axis=0)
            charges.append(jnp.where(lane < 64, block, moved))
        width = width_ref[domain_ref[0] * CL_DEV + cluster]
        node_x = const_ref[7] * width
        node_y = const_ref[4] * width
        node_z = const_ref[5] * width
        moments = [
            node_y * charges[2] - node_z * charges[1],
            node_z * charges[0] - node_x * charges[2],
            node_x * charges[1] - node_y * charges[0],
        ]
        order = [charges[0], charges[1], charges[2], charges[0], charges[1]] + moments
        for row, value in enumerate(order):
            for group in range(4):
                rows[row : row + 1, 128 * group : 128 * group + 128] = value[group : group + 1]
        high, low = split_bf16(rows[...])
        feature_ref[cluster] = jnp.concatenate([high, low], axis=0)

    @pl.loop(0, CL_DEV, step=2)
    def _(cluster):
        for extra in range(2):
            one_cluster(cluster + extra, rows_ref.at[extra])


def kernel_blocks(width, target_x, square_yz, group_pair, lane_pair):
    highs, lows = [], []
    for lanes in (2 * lane_pair, 2 * lane_pair + 1):
        high_rows, low_rows = [], []
        for group in (2 * group_pair, 2 * group_pair + 1):
            for half in range(2):
                apart_x = target_x[lanes] - width * node_list[group + 4 * half]
                square_x = apart_x * apart_x
                for b in range(0, NODES, 2):
                    pair = []
                    for square in square_yz[b : b + 2]:
                        inverse = lax.rsqrt(square + square_x)
                        pair.append(inverse * inverse * inverse)
                    high, low = split_bf16(jnp.concatenate(pair, axis=0))
                    high_rows.append(high)
                    low_rows.append(low)
        highs.append(jnp.concatenate(high_rows, axis=0))
        lows.append(jnp.concatenate(low_rows, axis=0))
    return jnp.concatenate(highs, axis=1), jnp.concatenate(lows, axis=1)


def tile_kernel(domain_ref, request_ref, place_ref, feature_ref, const_ref, out_ref, order_ref):
    sublane = lax.broadcasted_iota(jnp.int32, (8, 128), 0)

    def collect(peer, count):
        order_ref[count] = peer
        return count + (request_ref[peer, 0, 0] > 0).astype(jnp.int32)

    total = lax.fori_loop(0, DOMAINS, collect, 0)
    last = order_ref[jnp.maximum(total - 1, 0)]
    for extra in range(GROUP - 1):
        order_ref[total + extra] = last
    domain = domain_ref[0]

    def one_tile(peer):
        local_id = request_ref[peer, 0, 0] - 1
        source = domain * CL_DEV + local_id
        target = request_ref[peer, 0, 1]
        source_width = place_ref[3, source]
        target_width = place_ref[3, target]
        shift = [place_ref[axis, target] - place_ref[axis, source] for axis in range(3)]
        target_x = [const_ref[group] * target_width + shift[0] for group in range(4)]
        target_y = const_ref[4] * target_width + shift[1]
        target_z = const_ref[5] * target_width + shift[2]
        apart_z = target_z - const_ref[6] * source_width
        square_z = apart_z * apart_z + smoothing_sq
        square_yz = []
        for b in range(NODES):
            apart_y = target_y - source_width * node_list[b]
            square_yz.append(square_z + apart_y * apart_y)
        feature = feature_ref[local_id]
        for lane_pair in range(2):
            summed = None
            for group_pair in range(2):
                columns = feature[:, 256 * group_pair : 256 * group_pair + 256]
                for block in kernel_blocks(
                    source_width, target_x, square_yz, group_pair, lane_pair
                ):
                    product = jnp.dot(columns, block, preferred_element_type=jnp.float32)
                    summed = product if summed is None else summed + product
            summed = summed[:8] + summed[8:]
            for side in range(2):
                lanes = 2 * lane_pair + side
                block = summed[:, 128 * side : 128 * side + 128]
                first = jnp.where(
                    sublane == 0, target_y, jnp.where(sublane == 1, target_z, target_x[lanes])
                )
                second = jnp.where(
                    sublane == 0, target_z, jnp.where(sublane == 1, target_x[lanes], target_y)
                )
                velocity = (
                    first * pltpu.roll(block, 6, 0)
                    - second * pltpu.roll(block, 7, 0)
                    - pltpu.roll(block, 3, 0)
                )
                for c in range(3):
                    out_ref[peer * 12 + c * 4 + lanes] = velocity[c : c + 1]

    @pl.loop(0, (total + GROUP - 1) // GROUP)
    def _(step):
        for extra in range(GROUP):
            one_tile(order_ref[step * GROUP + extra])


def relay_kernel(order_ref, in_ref, out_ref, semaphore):
    @pl.loop(0, DOMAINS, step=8)
    def _(first):
        for extra in range(8):
            peer = first + extra
            pltpu.make_async_copy(
                in_ref.at[pl.ds(order_ref[peer] * 12, 12)],
                out_ref.at[pl.ds(peer * 12, 12)],
                semaphore,
            ).start()

    pltpu.make_async_copy(in_ref, out_ref, semaphore).wait()


def downward_kernel(owner_ref, part_ref, basis_ref, out_ref, proxy_ref):
    owner = owner_ref[...]
    column = lax.broadcasted_iota(jnp.int32, (DOMAINS, CL_DEV), 1)
    assign = (owner == column + 1).astype(jnp.bfloat16)
    alive = jnp.broadcast_to(owner > 0, (DOMAINS, 128))
    gather = functools.partial(
        lax.dot_general,
        dimension_numbers=(((0,), (0,)), ((), ())),
        preferred_element_type=jnp.float32,
    )
    for chunk in range(12):
        part = jnp.where(alive, part_ref[pl.ds(chunk, DOMAINS, stride=12), :], 0.0)
        high, low = split_bf16(part)
        proxy_ref[chunk * CL_DEV : (chunk + 1) * CL_DEV] = gather(assign, high) + gather(
            assign, low
        )

    def one_cluster(cluster):
        where = pl.ds(pl.multiple_of(cluster * PTS, PTS), PTS)
        rows = proxy_ref[pl.ds(cluster, 12, stride=CL_DEV), :]
        near, far = rows[:, :64], rows[:, 64:]
        left = jnp.concatenate(
            [piece[4 * c : 4 * c + 4] for c in range(3) for piece in (near, far)], axis=0
        )
        left_high, left_low = split_bf16(left)
        paired_high, paired_low = split_bf16(
            paired_rows(basis_ref[8:16, where], basis_ref[16:24, where])
        )
        spread = jnp.dot(
            jnp.concatenate([left_high, left_low, left_high], axis=1),
            jnp.concatenate([paired_high, paired_high, paired_low], axis=0),
            preferred_element_type=jnp.float32,
        )
        basis_x = basis_ref[0:8, where]
        for c in range(3):
            out_ref[c : c + 1, where] = jnp.sum(
                spread[8 * c : 8 * c + 8] * basis_x, axis=0, keepdims=True
            )

    @pl.loop(0, CL_DEV, step=2)
    def _(cluster):
        one_cluster(cluster)
        one_cluster(cluster + 1)


def in_vmem():
    return pl.BlockSpec(memory_space=pltpu.VMEM)


def in_smem():
    return pl.BlockSpec(memory_space=pltpu.SMEM)


def exchange(value):
    return lax.all_to_all(value, AXES, split_axis=0, concat_axis=0, tiled=True)


def settings(mebibytes):
    return pltpu.CompilerParams(vmem_limit_bytes=mebibytes << 20)


def local(point_coords, strengths, centers, half_widths, tile_source, tile_target, tile_count):
    domain = lax.axis_index(AXES).reshape(1)
    const = jnp.asarray(CONSTANTS)
    message = pl.pallas_call(
        message_kernel,
        out_shape=jax.ShapeDtypeStruct((DOMAINS, 128), jnp.int32),
        in_specs=[in_smem(), in_vmem(), in_vmem()],
        out_specs=in_vmem(),
        name="message",
    )(tile_count, tile_source, tile_target)
    received = exchange(message.reshape(DOMAINS, 1, 128))

    features, places, kept_const = pl.pallas_call(
        upward_kernel,
        out_shape=(
            jax.ShapeDtypeStruct((CL_DEV, 16, 512), jnp.bfloat16),
            jax.ShapeDtypeStruct((4, centers.shape[1]), jnp.float32),
            jax.ShapeDtypeStruct(const.shape, jnp.float32),
        ),
        in_specs=[in_smem(), in_smem()] + [in_vmem()] * 5,
        out_specs=(in_vmem(), in_vmem(), in_vmem()),
        scratch_shapes=[pltpu.VMEM((2, 8, 512), jnp.float32)],
        compiler_params=settings(8),
        cost_estimate=pl.CostEstimate(flops=10**8, bytes_accessed=10**6, transcendentals=0),
        name="upward",
    )(domain, half_widths, point_coords, strengths, const, centers, half_widths[None, :])

    parts = pl.pallas_call(
        tile_kernel,
        out_shape=jax.ShapeDtypeStruct((DOMAINS * 12, 1, 128), jnp.float32),
        in_specs=[in_smem(), in_smem(), in_smem(), in_vmem(), in_vmem()],
        out_specs=in_vmem(),
        scratch_shapes=[pltpu.SMEM((DOMAINS + GROUP,), jnp.int32)],
        compiler_params=settings(8),
        name="tiles",
    )(domain, received, places, features, kept_const)

    relayed = exchange(parts.reshape(DOMAINS, 1, 1536))
    alive = jnp.arange(TILES_DEV) < tile_count[0]
    from_target = (jnp.arange(DOMAINS)[:, None] == (tile_target[0] // CL_DEV)[None, :]) & alive
    relay_order = jnp.sum(jnp.where(from_target, (tile_source[0] // CL_DEV)[None, :], 0), axis=1)
    ordered = pl.pallas_call(
        relay_kernel,
        out_shape=jax.ShapeDtypeStruct((DOMAINS * 12, 1, 128), jnp.float32),
        in_specs=[in_smem(), in_vmem()],
        out_specs=pl.BlockSpec(memory_space=pl.ANY),
        scratch_shapes=[pltpu.SemaphoreType.DMA],
        compiler_params=settings(4),
        name="relay",
    )(relay_order, relayed.reshape(DOMAINS * 12, 1, 128))
    arrived = exchange(ordered.reshape(DOMAINS, 1, 1536))

    basis = pl.pallas_call(
        basis_kernel,
        out_shape=jax.ShapeDtypeStruct((24, CL_DEV * PTS), jnp.float32),
        in_specs=[in_vmem()],
        out_specs=in_vmem(),
        compiler_params=settings(8),
        cost_estimate=pl.CostEstimate(flops=10**8, bytes_accessed=2 * 10**6, transcendentals=0),
        name="basis",
    )(point_coords)
    owners = received[:, 0, 2:3]
    return pl.pallas_call(
        downward_kernel,
        out_shape=jax.ShapeDtypeStruct((3, CL_DEV * PTS), jnp.float32),
        in_specs=[in_vmem(), in_vmem(), in_vmem()],
        out_specs=in_vmem(),
        scratch_shapes=[pltpu.VMEM((12 * CL_DEV, 128), jnp.float32)],
        compiler_params=settings(8),
        name="downward",
    )(owners, arrived.reshape(DOMAINS * 12, 128), basis)


def solution(mesh):
    return jax.shard_map(
        local,
        mesh=mesh,
        in_specs=(
            P(None, AXES),
            P(None, AXES),
            P(),
            P(),
            P(AXES, None),
            P(AXES, None),
            P(AXES),
        ),
        out_specs=P(None, AXES),
        check_vma=False,
    )
```

time: 127 us -> 99.2 us (0.78)
  Pallas kernels: 55.4 us -> 35.2 us
  starting transfers between devices: 31.3 us -> 26 us
  local copies, waits for them, and re-layouts: 7.56 us -> 4.32 us
  waiting for transfers between devices: 30.4 us -> 32.1 us
    pallas_call x1, Pallas kernels: 37.9 us -> 21.8 us  [local(): pl.pallas_call(tile_kernel, out_shape=jax.ShapeDtypeStruct((DOMAINS * 12,...]
    all_to_all x3, starting transfers between devices: 31.3 us -> 26 us  [exchange(): return lax.all_to_all(value, AXES, split_axis=0, concat_axis=0, tiled=True)]
    slice x1, local copies, waits for them, and re-layouts: 3.09 us -> 0.2 us  [local(): owners = received[:, 0, 2:3]]
    pallas_call x0 -> x2, Pallas kernels: none -> 2.78 us  [the longest x1 1.47 us: local(): pl.pallas_call(message_kernel, out_shape=jax.ShapeDtypeStruct((DOMAINS, 1...]
    pallas_call x1, Pallas kernels: 6.99 us -> 4.31 us  [local(): pl.pallas_call(downward_kernel, out_shape=jax.ShapeDtypeStruct((3, CL_DEV...]
    pallas_call x1, Pallas kernels: 7.34 us -> 4.68 us  [local(): pl.pallas_call(upward_kernel, out_shape=(jax.ShapeDtypeStruct((CL_DEV, 16...]
    all_to_all x3, waiting for transfers between devices: 30.4 us -> 32.1 us  [exchange(): return lax.all_to_all(value, AXES, split_axis=0, concat_axis=0, tiled=True)]
    unnamed x8 -> x16, local copies, waits for them, and re-layouts: 2.4 us -> 4.12 us
  transfers between devices with their start and end apart: 3 -> 3, of which waited for: 3 -> 3; matrix products, arithmetic and copies ran while one was open for 4% -> 0% of each run, Pallas kernels for 6% -> 6%
where the time goes in v2:
time: 99.2 us; the launch traced here: 98.5 us
  Pallas kernels  35.2 us (35%)
  waiting for transfers between devices  32.1 us (32%)
  starting transfers between devices  26 us (26%)
  local copies, waits for them, and re-layouts  4.32 us (4%)
    all_to_all x3, waiting for transfers between devices, exchange(): return lax.all_to_all(value, AXES, split_axis=0, concat_axis=0, tiled=True)  32.1 us
    all_to_all x3, starting transfers between devices, exchange(): return lax.all_to_all(value, AXES, split_axis=0, concat_axis=0, tiled=True)  26 us
    pallas_call x1, Pallas kernels, local(): pl.pallas_call(tile_kernel, out_shape=jax.ShapeDtypeStruct((DOMAINS * 12,...  21.8 us
    pallas_call x1, Pallas kernels, local(): pl.pallas_call(upward_kernel, out_shape=(jax.ShapeDtypeStruct((CL_DEV, 16...  4.68 us
    pallas_call x1, Pallas kernels, local(): pl.pallas_call(downward_kernel, out_shape=jax.ShapeDtypeStruct((3, CL_DEV...  4.31 us
    unnamed x16, local copies, waits for them, and re-layouts  4.12 us
  transfers between devices with their start and end apart: 3, of which 3 were waited for; matrix products, arithmetic and copies ran while one was open for 0% of the time, Pallas kernels for 6%

profile of v2, /device:TPU:1, one launch (start us, length us, event | category | flops | bytes accessed | tf_op | source)
XLA Modules:
  0.0 98.5 jit_solution(10365792833957745938)
XLA Ops:
  0.7 1.5 %message.1 = s32[128,128]{1,0:T(8,128)} custom-call(s32[1]{0:T(128)} %copy.17.count_ref, s32[1,128]{1,0:T(1,128)} %source_ref.1, s32[1,128]{1,0:T(1,128)} %target_ref.1), custom_call_target="tpu_custom_call" | custom-call | tf_op jit(solution)/shard_map/message/pallas_call | solution.py:316
  2.1 11.5 %all-to-all-start = ((s32[128,1,128]{2,1,0:T(1,128)}), s32[128,1,128]{2,1,0:T(1,128)S(1)}, u32[]{:S(2)}, u32[]{:S(2)}) async-start(s32[128,1,128]{2,1,0:T(1,128)} %bitcast.18), calls=%async_computation | async-start | bytes 131072 | tf_op jit(solution)/shard_map/all_to_all | solution.py:306
  13.6 0.0 copy-start
  13.6 0.9 copy-done
  14.6 0.0 copy-start.2
  14.6 0.9 copy-done.2
  15.5 0.0 copy-start.3
  15.5 0.7 copy-done.3
  16.2 0.0 copy-start.4
  16.2 0.8 copy-done.4
  17.0 0.0 copy-start.5
  17.0 0.8 copy-done.5
  17.7 0.0 copy-start.6
  17.7 0.0 copy-start.7
  17.7 4.7 %upward.1 = (bf16[16,16,512]{2,1,0:T(8,128)(2,1)S(1)}, f32[4,2048]{1,0:T(4,128)S(1)}, f32[8,8,128]{2,1,0:T(8,128)S(1)}) custom-call(s32[1]{0:T(128)} %bitcast.5.domain_ref, f32[2048]{0:T(1024)S(1)} %copy-done.3, f32[3,16384]{1,0:T(4,128)S(1)} %copy-done, f32[3,16384]{1,0:T(4,128)S(1)} %copy-done.2, f32[8,8,128]{2,1,0:T(8,128)S(1)} %copy-done.5, ...), custom_call_target="tpu_custom_call" | custom-call | flops 100000000 | bytes 1000000 | tf_op jit(solution)/shard_map/upward/pallas_call | solution.py:325
  22.4 0.7 all-to-all-done.request_ref
  23.1 21.8 %tiles.1 = f32[1536,1,128]{2,1,0:T(1,128)} custom-call(s32[1]{0:T(128)} %bitcast.5.domain_ref, s32[128,1,128]{2,1,0:T(1,128)S(1)} %all-to-all-done.request_ref, f32[4,2048]{1,0:T(4,128)S(1)} %get-tuple-element.8.place_ref, bf16[16,16,512]{2,1,0:T(8,128)(2,1)S(1)} %get-tuple-element.9.feature_ref, f32[8,8,128]{2,1,0:T(8,128)S(1)} %get-tuple-element.10.const_ref), custom_call_target="tpu_custom_call" | custom-call | tf_op jit(solution)/shard_map/tiles/pallas_call | solution.py:340
  44.9 10.2 %all-to-all-start.1 = ((f32[128,1,1536]{2,1,0:T(1,128)}), f32[128,1,1536]{2,1,0:T(1,128)S(1)}, u32[]{:S(2)}, u32[]{:S(2)}) async-start(f32[128,1,1536]{2,1,0:T(1,128)} %bitcast.7), calls=%async_computation.1 | async-start | bytes 1572864 | tf_op jit(solution)/shard_map/all_to_all | solution.py:306
  55.2 0.0 copy-done.6
  55.2 0.0 copy-done.7
  55.2 0.1 select_reduce_fusion.order_ref
  55.3 16.3 %all-to-all-done.1 = f32[128,1,1536]{2,1,0:T(1,128)S(1)} async-done(((f32[128,1,1536]{2,1,0:T(1,128)}), f32[128,1,1536]{2,1,0:T(1,128)S(1)}, u32[]{:S(2)}, u32[]{:S(2)}) %all-to-all-start.1) | async-done | bytes 786464 | tf_op jit(solution)/shard_map/all_to_all | solution.py:306
  71.6 0.0 copy-start.1
  71.6 1.6 %relay.1 = f32[1536,1,128]{2,1,0:T(1,128)} custom-call(s32[128]{0:T(128)S(1)} %select_reduce_fusion.order_ref, f32[1536,1,128]{2,1,0:T(1,128)S(1)} %bitcast.14), custom_call_target="tpu_custom_call" | custom-call | tf_op jit(solution)/shard_map/relay/pallas_call | solution.py:354
  73.3 4.3 %all-to-all-start.2 = ((f32[128,1,1536]{2,1,0:T(1,128)}), f32[128,1,1536]{2,1,0:T(1,128)S(1)}, u32[]{:S(2)}, u32[]{:S(2)}) async-start(f32[128,1,1536]{2,1,0:T(1,128)} %bitcast.9), calls=%async_computation.2 | async-start | bytes 1572864 | tf_op jit(solution)/shard_map/all_to_all | solution.py:306
  77.6 0.0 copy-done.1
  77.6 1.3 %basis.1.basis_ref = f32[24,16384]{1,0:T(8,128)S(1)} custom-call(f32[3,16384]{1,0:T(4,128)S(1)} %copy-done.1), custom_call_target="tpu_custom_call" | custom-call | flops 100000000 | bytes 2000000 | tf_op jit(solution)/shard_map/basis/pallas_call | solution.py:365
  78.9 0.2 slice.4
  79.1 15.1 %all-to-all-done.2 = f32[128,1,1536]{2,1,0:T(1,128)S(1)} async-done(((f32[128,1,1536]{2,1,0:T(1,128)}), f32[128,1,1536]{2,1,0:T(1,128)S(1)}, u32[]{:S(2)}, u32[]{:S(2)}) %all-to-all-start.2) | async-done | bytes 786464 | tf_op jit(solution)/shard_map/all_to_all | solution.py:306
  94.2 4.3 %downward.1 = f32[3,16384]{1,0:T(4,128)} custom-call(s32[128,1]{1,0:T(8,128)S(1)} %bitcast.16, f32[1536,128]{1,0:T(8,128)S(1)} %bitcast.15, f32[24,16384]{1,0:T(8,128)S(1)} %basis.1.basis_ref), custom_call_target="tpu_custom_call" | custom-call | tf_op jit(solution)/shard_map/downward/pallas_call | solution.py:375
  (2 shorter events, 0.0 us)
Async XLA Ops:
  2.1 21.0 %all-to-all-start = ((s32[128,1,128]{2,1,0:T(1,128)}), s32[128,1,128]{2,1,0:T(1,128)S(1)}, u32[]{:S(2)}, u32[]{:S(2)}) async-start(s32[128,1,128]{2,1,0:T(1,128)} %bitcast.18), calls=%async_computation | async-start | bytes 131072 | tf_op jit(solution)/shard_map/all_to_all | solution.py:306
  13.6 1.0 copy-start
  14.6 0.9 copy-start.2
  15.5 0.7 copy-start.3
  16.2 0.8 copy-start.4
  17.0 0.8 copy-start.5
  17.7 37.4 %copy-start.6 = (s32[1,128]{1,0:T(1,128)S(1)}, s32[1,128]{1,0:T(1,128)}, u32[]{:S(2)}) copy-start(s32[1,128]{1,0:T(1,128)} %source_ref.1) | copy-start | bytes 1540
  17.7 37.4 %copy-start.7 = (s32[1,128]{1,0:T(1,128)S(1)}, s32[1,128]{1,0:T(1,128)}, u32[]{:S(2)}) copy-start(s32[1,128]{1,0:T(1,128)} %target_ref.1) | copy-start | bytes 1540
  44.9 26.7 %all-to-all-start.1 = ((f32[128,1,1536]{2,1,0:T(1,128)}), f32[128,1,1536]{2,1,0:T(1,128)S(1)}, u32[]{:S(2)}, u32[]{:S(2)}) async-start(f32[128,1,1536]{2,1,0:T(1,128)} %bitcast.7), calls=%async_computation.1 | async-start | bytes 1572864 | tf_op jit(solution)/shard_map/all_to_all | solution.py:306
  71.6 6.0 %copy-start.1 = (f32[3,16384]{1,0:T(4,128)S(1)}, f32[3,16384]{1,0:T(4,128)}, u32[]{:S(2)}) copy-start(f32[3,16384]{1,0:T(4,128)} %coord_ref.3) | copy-start | bytes 589828
  73.3 21.0 %all-to-all-start.2 = ((f32[128,1,1536]{2,1,0:T(1,128)}), f32[128,1,1536]{2,1,0:T(1,128)S(1)}, u32[]{:S(2)}, u32[]{:S(2)}) async-start(f32[128,1,1536]{2,1,0:T(1,128)} %bitcast.9), calls=%async_computation.2 | async-start | bytes 1572864 | tf_op jit(solution)/shard_map/all_to_all | solution.py:306
